TPU v7x, 32 devices: a whole 2x2x4 slice. The times are simulated.
32 devices in a mesh: comp: 8 (over y, x, core), tile: 4 (over z).
Axes of the slice: x: 2, y: 2, z: 4, core: 2. Of those that a mesh axis runs over, the one named last changes fastest.
Arguments:
- spectrum: bfloat16 [1296, 128, 1024], P('comp', 'tile'), may hold values from 0.049804688 to 1
- courant_x: float32 [1296], replicated, may hold values from -0.45 to 0.45
- courant_y: float32 [1296], replicated, may hold values from -0.45 to 0.45
- growth: float32 [1296], replicated, may hold values from 0.02 to 0.2
- dissipation: float32 [1296], replicated, may hold values from 0.1 to 1
- bin_width: float32 [1296], replicated, may hold values from 0.00038580247 to 0.0030864198
- transfer: bfloat16 [1296, 1296], replicated, may hold values from -0.15625 to 0.15625
- stress_weights: float32 [2, 1296], replicated, may hold values from -0.15625 to 0.15625
- orbital_weights: float32 [1296], replicated, may hold values from 0.000154321 to 0.0015432099
- wind: float32 [128, 1024], P('tile', 'comp'), may hold values from 1 to 10
- wave_wet: int32 [128, 1024], P('tile', 'comp'), may hold values 0 or 1
- owner: int32 [4, 8, 32, 128, 1], P('tile', 'comp'), may hold values from 0 to 31; in each aligned block of 4096 rows (0 to 4095, 4096 to 8191, ..., all dimensions but the last counted through in order) at most 384 rows name the same one
- cell_index: int32 [4, 8, 32, 128], P('tile', 'comp'), may hold values from 0 to 2047
- current_stress: float32 [2, 64, 1024], P(None, 'tile', 'comp'), may hold values from -3 to 3
- sediment: float32 [4, 64, 1024], P(None, 'tile', 'comp'), may hold values from 0.1 to 2
- metals: float32 [4, 64, 1024], P(None, 'tile', 'comp'), may hold values from 0.1 to 2
- bed_class: int32 [64, 1024], P('tile', 'comp'), may hold values from 0 to 3
- roms_wet: int32 [64, 1024], P('tile', 'comp'), may hold values 0 or 1
- class_props: float32 [3, 4], replicated, may hold values from 0.2 to 0.8
- partition: float32 [4, 4], replicated, may hold values from 0.3 to 3
Outputs:
- spectrum_new: bfloat16 [1296, 128, 1024], P(None, 'tile', 'comp')
- sediment_new: float32 [4, 64, 1024], P(None, 'tile', 'comp')
- dissolved: float32 [4, 64, 1024], P(None, 'tile', 'comp')
- sorbed: float32 [4, 64, 1024], P(None, 'tile', 'comp')
Inputs may be any that keep to these rules, and one draw needn't show every extreme that they name: `owner`: within each aligned block of 4096 points (one device's points, in order), no tile is named more than 384 times, a bound that some block reaches.
All inputs are finite; a program needn't handle non-finite values. No bound on the sum of `wave_wet` or of `roms_wet` on one device may be relied on, other than what follows from the above.
Results may differ from a plain program's by a relative error of at most 0.0049.
Values may be sent and summed in bfloat16 or wider, within the bound.
A program may use at most 192 MiB of HBM per device.

v0:
```python
import jax
import jax.numpy as jnp
from jax import lax
from jax.sharding import PartitionSpec as P

WAVE_STEP = 0.5
SEDIMENT_STEP = 1.0
DIFFUSION = 0.2


def with_halo(cells, sides, width):
    for axis, dim in sides:
        count = lax.axis_size(axis)
        ends = count - 1
        head = lax.slice_in_dim(cells, 0, width, axis=dim)
        tail = lax.slice_in_dim(cells, cells.shape[dim] - width, cells.shape[dim], axis=dim)
        cells = jnp.concatenate(
            [
                lax.ppermute(tail, axis, [(i, (i + 1) % count) for i in range(ends)]),
                cells,
                lax.ppermute(head, axis, [((i + 1) % count, i) for i in range(ends)]),
            ],
            axis=dim,
        )
    return cells


def upwind(padded, speed_x, speed_y):
    centre = padded[..., 1:-1, 1:-1]
    north = padded[..., :-2, 1:-1]
    south = padded[..., 2:, 1:-1]
    west = padded[..., 1:-1, :-2]
    east = padded[..., 1:-1, 2:]
    return (
        centre
        - jnp.maximum(speed_x, 0.0) * (centre - north)
        - jnp.minimum(speed_x, 0.0) * (south - centre)
        - jnp.maximum(speed_y, 0.0) * (centre - west)
        - jnp.minimum(speed_y, 0.0) * (east - centre)
    )


def on_device(
    spectrum,
    courant_x,
    courant_y,
    growth,
    dissipation,
    bin_width,
    transfer,
    stress_weights,
    orbital_weights,
    wind,
    wave_wet,
    owner,
    cell_index,
    current_stress,
    sediment,
    metals,
    bed_class,
    roms_wet,
    class_props,
    partition,
):
    n_comp = lax.axis_size("comp")
    n_tile = lax.axis_size("tile")
    devices = n_comp * n_tile
    own_count = spectrum.shape[0]
    first = lax.axis_index("comp") * own_count
    speed_x = lax.dynamic_slice_in_dim(courant_x, first, own_count)
    speed_y = lax.dynamic_slice_in_dim(courant_y, first, own_count)
    rowed = with_halo(spectrum, (("tile", 1),), 1)
    padded = jnp.pad(rowed, ((0, 0), (0, 0), (1, 1)))
    stepped = upwind(
        padded.astype(jnp.float32), speed_x[:, None, None], speed_y[:, None, None]
    ).astype(jnp.bfloat16)
    block = lax.all_to_all(stepped, "comp", split_axis=2, concat_axis=0, tiled=True)
    energy_block = block.astype(jnp.float32)
    mixed = jnp.einsum("jk,krc->jrc", transfer, block, preferred_element_type=jnp.float32)
    total = jnp.einsum("k,krc->rc", bin_width, energy_block, precision=lax.Precision.HIGHEST)
    ratio = total / (total + 1.0)
    part = energy_block + WAVE_STEP * (
        mixed - dissipation[:, None, None] * ratio[None] * energy_block
    )
    part, arrived = (part, block)
    energy = arrived.astype(jnp.float32)
    relaxed = part + WAVE_STEP * growth[:, None, None] * wind[None] * energy
    fresh = wave_wet.astype(jnp.float32)[None] * jnp.maximum(relaxed, 0.0)
    spectrum_new = fresh.astype(jnp.bfloat16)
    weights_all = jnp.concatenate([stress_weights, orbital_weights[None, :]], axis=0)
    forces = jnp.einsum("sk,krc->src", weights_all, fresh, precision=lax.Precision.HIGHEST)
    points = forces.shape[1] * forces.shape[2]
    slots = max(2, 3 * points // devices)
    cells = sediment.shape[1] * sediment.shape[2]
    owner_flat = owner.reshape(points)
    cell_flat = cell_index.reshape(points)
    hits = (owner_flat[:, None] == jnp.arange(devices, dtype=jnp.int32)[None, :]).astype(jnp.int32)
    before_count = jnp.sum((jnp.cumsum(hits, axis=0) - hits) * hits, axis=1)
    target = owner_flat * slots + before_count
    packed = (
        jnp.zeros((3, devices * slots), jnp.float32).at[:, target].set(forces.reshape(3, points))
    )
    labels = jnp.full((devices * slots,), cells, jnp.int32).at[target].set(cell_flat)
    got_values, got_labels = (
        lax.all_to_all(
            packed.reshape(3, devices, slots).astype(jnp.bfloat16),
            ("comp", "tile"),
            split_axis=1,
            concat_axis=1,
            tiled=True,
        ).astype(jnp.float32),
        lax.all_to_all(
            labels.reshape(1, devices, slots),
            ("comp", "tile"),
            split_axis=1,
            concat_axis=1,
            tiled=True,
        ),
    )
    rows_here = sediment.shape[1]
    cols_here = sediment.shape[2]
    bottom = (
        jnp.zeros((3, cells), jnp.float32)
        .at[:, got_labels.reshape(-1)]
        .add(got_values.reshape(3, -1), mode="drop")
        .reshape(3, rows_here, cols_here)
    )
    shear_x = current_stress[0] + bottom[0]
    shear_y = current_stress[1] + bottom[1]
    shear = jnp.sqrt(shear_x * shear_x + shear_y * shear_y + bottom[2])
    classes_count = sediment.shape[0]
    low_share = 0.5 / classes_count
    high_share = 1.0 - (classes_count - 1) * low_share
    classes = jnp.arange(classes_count, dtype=jnp.int32)[:, None, None]
    fraction = jnp.where(bed_class[None] == classes, high_share, low_share)
    erosion = (
        class_props[0][:, None, None]
        * fraction
        * jnp.maximum(shear[None] / class_props[1][:, None, None] - 1.0, 0.0)
    )
    wetness = roms_wet.astype(jnp.float32)
    settled = wetness * (
        sediment + SEDIMENT_STEP * (erosion - class_props[2][:, None, None] * sediment)
    )
    carried = wetness * metals
    fields = jnp.concatenate([settled, carried], axis=0)
    edged = with_halo(fields, (("comp", 2), ("tile", 1)), 1)
    centre = edged[:, 1:-1, 1:-1]
    beside_all = edged[:, :-2, 1:-1] + edged[:, 2:, 1:-1] + edged[:, 1:-1, :-2] + edged[:, 1:-1, 2:]
    diffused = wetness * (centre + DIFFUSION * (beside_all - 4.0 * centre))
    sediment_new = diffused[:classes_count]
    spread = diffused[classes_count:]
    denominator = 1.0 + jnp.einsum(
        "ms,sxy->mxy", partition, sediment_new, precision=lax.Precision.HIGHEST
    )
    dissolved = spread / denominator
    sorbed = spread - dissolved
    return (spectrum_new, sediment_new, dissolved, sorbed)


def solution(mesh):
    in_specs = (
        P("comp", "tile", None),
        P(),
        P(),
        P(),
        P(),
        P(),
        P(),
        P(),
        P(),
        P("tile", "comp"),
        P("tile", "comp"),
        P("tile", "comp", None, None, None),
        P("tile", "comp", None, None),
        P(None, "tile", "comp"),
        P(None, "tile", "comp"),
        P(None, "tile", "comp"),
        P("tile", "comp"),
        P("tile", "comp"),
        P(),
        P(),
    )
    out_specs = (
        P(None, "tile", "comp"),
        P(None, "tile", "comp"),
        P(None, "tile", "comp"),
        P(None, "tile", "comp"),
    )
    return jax.shard_map(
        on_device, mesh=mesh, in_specs=in_specs, out_specs=out_specs, check_vma=False
    )
```

profile of v0, /device:TPU:11, one launch (start us, length us, event | category | flops | bytes accessed | tf_op | source)
XLA Modules:
  0.0 549.4 jit_solution(10726462506963610363)
XLA Ops:
  0.6 0.0 copy-start
  0.6 3.8 fusion.60
  4.5 0.1 copy.145
  4.6 3.2 collective-permute-start
  7.8 0.1 copy.146
  7.9 2.1 collective-permute-start.1
  10.0 25.1 %copy.130 = bf16[162,32,1024]{0,1,2:T(8,128)(2,1)} copy(bf16[162,32,1024]{2,1,0:T(8,128)(2,1)} %param.20) | data formatting | bytes 21233664 | tf_op args[0]
  35.1 0.8 dynamic-slice_maximum_fusion
  35.9 0.0 collective-permute-done
  35.9 0.8 copy.129
  36.7 0.0 collective-permute-done.1
  36.7 0.8 copy.131
  37.6 27.6 %fusion.20 = f32[162,34,1026]{0,1,2:T(8,128)} fusion(bf16[162,1,1024]{0,1,2:T(2,128)(2,1)S(1)} %copy.131, bf16[162,32,1024]{0,1,2:T(8,128)(2,1)} %copy.130, bf16[162,1,1024]{0,1,2:T(2,128)(2,1)S(1)} %copy.129), kind=kLoop, calls=%fused_computation.32 | loop fusion | flops 67814496 | bytes 33885216 | tf_op jit(solution)/shard_map/convert_element_type | solution.py:75
  65.2 68.6 %fusion.3 = bf16[162,32,1024]{0,1,2:T(8,128)(2,1)} fusion(f32[162,34,1026]{0,1,2:T(8,128)} %fusion.20, f32[162]{0:T(256)S(1)} %get-tuple-element.52, f32[162]{0:T(256)S(1)} %get-tuple-element.51, f32[162]{0:T(256)S(1)} %get-tuple-element.58, f32[162]{0:T(256)S(1)} %get-tuple-element.59), kind=kLoop, calls=%fused_computation.9 | loop fusion | flops 69009408 | bytes 116787744 | tf_op jit(solution)/shard_map/convert_element_type | solution.py:76
  133.8 0.0 copy-start.1
  133.8 0.0 copy-start.11
  133.8 0.0 copy-start.13
  133.9 0.0 copy-start.12
  133.9 7.1 %all-to-all-start = ((bf16[162,32,1024]{0,1,2:T(8,128)(2,1)}), bf16[162,32,1024]{0,1,2:T(8,128)(2,1)}, u32[]{:S(2)}, u32[]{:S(2)}) async-start(bf16[162,32,1024]{0,1,2:T(8,128)(2,1)} %fusion.3), calls=%async_computation | async-start | bytes 33554432 | tf_op jit(solution)/shard_map/all_to_all | solution.py:77
  141.1 0.1 fusion.32
  141.1 9.2 %reduce-window.6 = s32[32,32,128]{2,1,0:T(8,128)S(1)} reduce-window(s32[32,32,128]{2,1,0:T(8,128)S(1)} %fusion.32, s32[]{:T(128)} %constant.21.clone.1), window={size=1x1x128 pad=0_0x0_0x127_0}, to_apply=%region_0.1 | reduce-window | flops 16646144 | bytes 1048580 | tf_op jit(solution)/shard_map/reduce-window
  150.4 0.8 slice_reduce_fusion.3
  151.2 0.2 reduce-window.9
  151.4 0.2 broadcast_add_fusion
  151.6 0.4 fusion.29
  152.0 16.3 %scatter_custom_fusion = s32[12288]{0:T(1024)} fusion(s32[4096]{0:T(1024)S(1)} %bitcast.104, s32[4096]{0:T(1024)} %bitcast.106, s32[]{:T(128)} %constant.11.clone.1), kind=kCustom, calls=%fused_computation.95 | custom fusion | bytes 49664 | tf_op jit(solution)/shard_map/scatter | solution.py:103
  168.3 155.2 %all-to-all-done = bf16[162,32,1024]{0,1,2:T(8,128)(2,1)} async-done(((bf16[162,32,1024]{0,1,2:T(8,128)(2,1)}), bf16[162,32,1024]{0,1,2:T(8,128)(2,1)}, u32[]{:S(2)}, u32[]{:S(2)}) %all-to-all-start) | async-done | bytes 10616864 | tf_op jit(solution)/shard_map/all_to_all | solution.py:77
  323.5 5.5 all-to-all-start.1
  329.0 0.0 copy-start.14
  329.0 0.0 copy-start.15
  329.0 24.3 %copy.133 = bf16[8,162,32,128]{3,2,1,0:T(8,128)(2,1)} copy(bf16[8,162,32,128]{1,2,3,0:T(8,128)(2,1)} %bitcast.2) | data formatting | bytes 21233664 | tf_op jit(solution)/shard_map/all_to_all | solution.py:77
  353.3 12.8 %fusion.21 = f32[1,32,128]{2,0,1:T(1,128)S(1)} fusion(f32[1296,1,1]{0,1,2:T(1,128)S(1)} %reshape.165, bf16[1296,32,128]{2,1,0:T(8,128)(2,1)} %bitcast.92), kind=kOutput, calls=%fused_computation.33 | convolution fusion | flops 63700992 | bytes 10638400 | tf_op jit(solution)/shard_map/k,krc->rc/dot_general | solution.py:80
  366.1 0.0 copy-start.7
  366.1 30.0 %fusion.61 = (bf16[1296,32,128]{2,0,1:T(8,128)(2,1)}, f32[1296,32,128]{2,0,1:T(8,128)}) fusion(f32[32,128]{1,0:T(8,128)S(1)} %copy-done.14, f32[1296]{0:T(1024)S(1)} %broadcast_multiply_fusion.1, f32[32,128]{1,0:T(8,128)S(1)} %add_divide_fusion, f32[1296]{0:T(1024)S(1)} %copy-done.15, bf16[1296,32,128]{2,1,0:T(8,128)(2,1)} %bitcast.93, ...), kind=kOutput, calls=%fused_computation.126 | convolution fusion | flops 13823115264 | bytes 45886080 | tf_op jit(solution)/shard_map/jk,krc->jrc/dot_general | solution.py:79
  396.1 16.7 %convolution_bitcast_fusion = f32[4096,3]{0,1:T(4,128)S(1)} fusion(f32[1296,32,128]{2,0,1:T(8,128)} %get-tuple-element.57, f32[1,1296]{1,0:T(1,128)S(1)} %broadcast_in_dim.16, f32[2,1296]{1,0:T(2,128)S(1)} %copy-done.7), kind=kOutput, calls=%fused_computation.36 | convolution fusion | flops 191106864 | bytes 21298368 | tf_op jit(solution)/shard_map/sk,krc->src/dot_general | solution.py:91
  412.8 0.0 copy-start.4
  412.8 0.0 copy-start.8
  412.8 0.6 copy.136
  413.5 13.7 %scatter_custom_fusion.1 = f32[3,12288]{0,1:T(8,128)} fusion(s32[4096]{0:T(1024)S(1)} %bitcast.105, f32[4096,3]{1,0:T(8,128)S(1)} %copy.136, f32[]{:T(128)} %constant.23.clone.1), kind=kCustom, calls=%fused_computation.38 | custom fusion | bytes 147460 | tf_op jit(solution)/shard_map/scatter | solution.py:101
  427.1 3.0 convert_element_type.43
  430.2 2.2 copy.137
  432.3 0.0 all-to-all-done.1
  432.3 5.8 %all-to-all-start.2 = ((bf16[3,32,384]{2,0,1:T(4,128)(2,1)}), bf16[3,32,384]{2,0,1:T(4,128)(2,1)S(1)}, u32[]{:S(2)}, u32[]{:S(2)}) async-start(bf16[3,32,384]{2,0,1:T(4,128)(2,1)} %copy.137), calls=%async_computation.2 | async-start | bytes 196608 | tf_op jit(solution)/shard_map/all_to_all | solution.py:105
  438.2 0.1 compare_select_fusion
  438.2 5.6 %all-to-all-done.2 = bf16[3,32,384]{2,0,1:T(4,128)(2,1)S(1)} async-done(((bf16[3,32,384]{2,0,1:T(4,128)(2,1)}), bf16[3,32,384]{2,0,1:T(4,128)(2,1)S(1)}, u32[]{:S(2)}, u32[]{:S(2)}) %all-to-all-start.2) | async-done | bytes 73760 | tf_op jit(solution)/shard_map/all_to_all | solution.py:105
  443.8 4.0 copy.138
  447.8 66.2 %scatter_custom_fusion.2 = f32[3,2048]{0,1:T(8,128)S(1)} fusion(s32[12288]{0:T(1024)S(1)} %bitcast.103, f32[12288,3]{1,0:T(8,128)} %copy.138, f32[]{:T(128)} %constant.23.clone.1), kind=kCustom, calls=%fused_computation.50 | custom fusion | flops 36864 | bytes 25088 | tf_op jit(solution)/shard_map/scatter-add | solution.py:125
  514.0 1.4 slice_reduce_fusion.2
  515.5 0.1 broadcast_multiply_fusion
  515.6 0.1 fusion.33
  515.7 3.3 collective-permute-start.2
  518.9 1.9 collective-permute-start.3
  520.9 0.0 collective-permute-done.2
  520.9 4.5 collective-permute-done.3
  525.4 0.1 pad_maximum_fusion.16
  525.5 2.5 collective-permute-start.4
  528.0 2.8 collective-permute-start.5
  530.8 17.1 %copy.141 = bf16[1296,32,128]{2,1,0:T(8,128)(2,1)} copy(bf16[1296,32,128]{2,0,1:T(8,128)(2,1)} %get-tuple-element.56) | data formatting | bytes 21233664
  547.9 0.0 collective-permute-done.4
  547.9 0.0 collective-permute-done.5
  547.9 0.2 fusion.39
  548.1 0.0 copy-start.2
  548.1 0.2 fusion.47
  548.3 0.6 slice_subtract_fusion.4
  (32 shorter events, 0.1 us)
Async XLA Ops:
  0.6 547.5 %copy-start = (f32[4,4]{1,0:T(4,128)S(1)}, f32[4,4]{1,0:T(4,128)}, u32[]{:S(2)}) copy-start(f32[4,4]{1,0:T(4,128)} %param.39) | copy-start | bytes 196
  4.6 31.3 %collective-permute-start = (bf16[162,1,1024]{2,0,1:T(8,128)(2,1)S(1)}, bf16[162,1,1024]{2,0,1:T(8,128)(2,1)S(1)}, u32[]{:S(2)}, u32[]{:S(2)}) collective-permute-start(bf16[162,1,1024]{2,0,1:T(8,128)(2,1)S(1)} %copy.145), channel_id=1, source_target_pairs={{0,1},{1,2},{2,3},{4,5},{5,6},{6,7},{8,9},{9,10},{10,11},{12,13},{... | collective-permute-start | bytes 995336 | tf_op jit(solution)/shard_map/ppermute | solution.py:19
  7.9 28.8 %collective-permute-start.1 = (bf16[162,1,1024]{2,0,1:T(8,128)(2,1)S(1)}, bf16[162,1,1024]{2,0,1:T(8,128)(2,1)S(1)}, u32[]{:S(2)}, u32[]{:S(2)}) collective-permute-start(bf16[162,1,1024]{2,0,1:T(8,128)(2,1)S(1)} %copy.146), channel_id=1, source_target_pairs={{1,0},{2,1},{3,2},{5,4},{6,5},{7,6},{9,8},{10,9},{11,10},{13,12},{... | collective-permute-start | bytes 995336 | tf_op jit(solution)/shard_map/ppermute | solution.py:21
  133.8 7.2 %copy-start.9 = (f32[1296]{0:T(1024)S(1)}, f32[1296]{0:T(1024)}, u32[]{:S(2)}) copy-start(f32[1296]{0:T(1024)} %param.25) | copy-start | bytes 15556
  133.8 7.2 %copy-start.6 = (s32[32,128]{1,0:T(8,128)S(1)}, s32[32,128]{1,0:T(8,128)}, u32[]{:S(2)}) copy-start(s32[32,128]{1,0:T(8,128)} %param.30) | copy-start | bytes 49156
  133.8 7.2 %copy-start.10 = (f32[1296]{0:T(1024)S(1)}, f32[1296]{0:T(1024)}, u32[]{:S(2)}) copy-start(f32[1296]{0:T(1024)} %param.28) | copy-start | bytes 15556
  133.8 7.3 %copy-start.1 = (s32[1,1,32,128,1]{3,4,2,1,0:T(1,128)S(1)}, s32[1,1,32,128,1]{3,4,2,1,0:T(1,128)}, u32[]{:S(2)}) copy-start(s32[1,1,32,128,1]{3,4,2,1,0:T(1,128)} %param.31) | copy-start | bytes 49156
  133.8 17.5 %copy-start.11 = (s32[16,128]{1,0:T(8,128)S(1)}, s32[16,128]{1,0:T(8,128)}, u32[]{:S(2)}) copy-start(s32[16,128]{1,0:T(8,128)} %param.37) | copy-start | bytes 24580
  133.8 34.4 %copy-start.13 = (f32[3,4]{1,0:T(4,128)S(1)}, f32[3,4]{1,0:T(4,128)}, u32[]{:S(2)}) copy-start(f32[3,4]{1,0:T(4,128)} %param.38) | copy-start | bytes 148
  133.9 34.4 %copy-start.12 = (f32[1296]{0:T(1024)S(1)}, f32[1296]{0:T(1024)}, u32[]{:S(2)}) copy-start(f32[1296]{0:T(1024)} %param.23) | copy-start | bytes 15556
  133.9 189.6 %all-to-all-start = ((bf16[162,32,1024]{0,1,2:T(8,128)(2,1)}), bf16[162,32,1024]{0,1,2:T(8,128)(2,1)}, u32[]{:S(2)}, u32[]{:S(2)}) async-start(bf16[162,32,1024]{0,1,2:T(8,128)(2,1)} %fusion.3), calls=%async_computation | async-start | bytes 33554432 | tf_op jit(solution)/shard_map/all_to_all | solution.py:77
  323.5 108.8 %all-to-all-start.1 = ((s32[1,32,384]{2,0,1:T(1,128)}), s32[1,32,384]{2,0,1:T(1,128)S(1)}, u32[]{:S(2)}, u32[]{:S(2)}) async-start(s32[1,32,384]{2,0,1:T(1,128)} %bitcast.17), calls=%async_computation.1 | async-start | bytes 98304 | tf_op jit(solution)/shard_map/all_to_all | solution.py:112
  329.0 37.1 %copy-start.14 = (f32[32,128]{1,0:T(8,128)S(1)}, f32[32,128]{1,0:T(8,128)}, u32[]{:S(2)}) copy-start(f32[32,128]{1,0:T(8,128)} %param.29) | copy-start | bytes 49156
  329.0 37.1 %copy-start.15 = (f32[1296]{0:T(1024)S(1)}, f32[1296]{0:T(1024)}, u32[]{:S(2)}) copy-start(f32[1296]{0:T(1024)} %param.24) | copy-start | bytes 15556
  366.1 30.0 %copy-start.7 = (f32[2,1296]{1,0:T(2,128)S(1)}, f32[2,1296]{1,0:T(2,128)}, u32[]{:S(2)}) copy-start(f32[2,1296]{1,0:T(2,128)} %param.27) | copy-start | bytes 31108
  412.8 102.7 %copy-start.5 = (f32[2,16,128]{2,1,0:T(8,128)S(1)}, f32[2,16,128]{2,1,0:T(8,128)}, u32[]{:S(2)}) copy-start(f32[2,16,128]{2,1,0:T(8,128)} %param.33) | copy-start | bytes 49156
  412.8 102.7 %copy-start.3 = (f32[4,16,128]{2,1,0:T(8,128)S(1)}, f32[4,16,128]{2,1,0:T(8,128)}, u32[]{:S(2)}) copy-start(f32[4,16,128]{2,1,0:T(8,128)} %param.35) | copy-start | bytes 98308
  412.8 102.7 %copy-start.4 = (f32[4,16,128]{2,1,0:T(8,128)S(1)}, f32[4,16,128]{2,1,0:T(8,128)}, u32[]{:S(2)}) copy-start(f32[4,16,128]{2,1,0:T(8,128)} %param.34) | copy-start | bytes 98308
  412.8 102.7 %copy-start.8 = (s32[16,128]{1,0:T(8,128)S(1)}, s32[16,128]{1,0:T(8,128)}, u32[]{:S(2)}) copy-start(s32[16,128]{1,0:T(8,128)} %param.36) | copy-start | bytes 24580
  432.3 11.5 %all-to-all-start.2 = ((bf16[3,32,384]{2,0,1:T(4,128)(2,1)}), bf16[3,32,384]{2,0,1:T(4,128)(2,1)S(1)}, u32[]{:S(2)}, u32[]{:S(2)}) async-start(bf16[3,32,384]{2,0,1:T(4,128)(2,1)} %copy.137), calls=%async_computation.2 | async-start | bytes 196608 | tf_op jit(solution)/shard_map/all_to_all | solution.py:105
  515.7 5.2 collective-permute-start.2
  518.9 6.5 %collective-permute-start.3 = (f32[8,16,1]{2,1,0:T(8,128)S(1)}, f32[8,16,1]{2,1,0:T(8,128)S(1)}, u32[]{:S(2)}, u32[]{:S(2)}) collective-permute-start(f32[8,16,1]{2,1,0:T(8,128)S(1)} %get-tuple-element.46), channel_id=1, source_target_pairs={{4,0},{8,4},{12,8},{16,12},{20,16},{24,20},{28,24},{5,1},{9,5},{13... | collective-permute-start | bytes 1544 | tf_op jit(solution)/shard_map/ppermute | solution.py:21
  525.5 22.4 %collective-permute-start.4 = (f32[8,1,130]{2,1,0:T(1,128)S(1)}, f32[8,1,130]{2,1,0:T(1,128)S(1)}, u32[]{:S(2)}, u32[]{:S(2)}) collective-permute-start(f32[8,1,130]{2,1,0:T(1,128)S(1)} %get-tuple-element.43), channel_id=1, source_target_pairs={{0,1},{1,2},{2,3},{4,5},{5,6},{6,7},{8,9},{9,10},{10,11},{12,13},{... | collective-permute-start | bytes 12488 | tf_op jit(solution)/shard_map/ppermute | solution.py:19
  528.0 19.9 %collective-permute-start.5 = (f32[8,1,130]{2,1,0:T(1,128)S(1)}, f32[8,1,130]{2,1,0:T(1,128)S(1)}, u32[]{:S(2)}, u32[]{:S(2)}) collective-permute-start(f32[8,1,130]{2,1,0:T(1,128)S(1)} %get-tuple-element.44), channel_id=1, source_target_pairs={{1,0},{2,1},{3,2},{5,4},{6,5},{7,6},{9,8},{10,9},{11,10},{13,12},{... | collective-permute-start | bytes 12488 | tf_op jit(solution)/shard_map/ppermute | solution.py:21
  548.1 0.8 copy-start.2
where the time goes:
time: 559 us; the launch traced here: 549 us
  other arithmetic  178 us (32%)
  waiting for transfers between devices  165 us (30%)
  local copies, waits for them, and re-layouts  111 us (20%)
  matrix products  59.6 us (11%)
  starting transfers between devices  34.2 us (6%)
    all_to_all x1, waiting for transfers between devices, on_device(): lax.all_to_all(stepped, 'comp', split_axis=2, concat_axis=0, tiled=True)  155 us
    convert_element_type x1, other arithmetic, on_device(): stepped = upwind(padded.astype(jnp.float32), speed_x[:, None, None], spee...  68.6 us
    scatter-add x1, other arithmetic, on_device(): bottom = jnp.zeros((3, cells), jnp.float32).at[:, got_labels.reshape(-1)]...  66.2 us
    unnamed x37, local copies, waits for them, and re-layouts  42.4 us
    dot_general x1, matrix products, on_device(): jnp.einsum('jk,krc->jrc', transfer, block, preferred_element_type=jnp.flo...  30 us
    convert_element_type x1, other arithmetic, on_device(): padded.astype(jnp.float32)  27.6 us
    all_to_all x1, local copies, waits for them, and re-layouts, on_device(): lax.all_to_all(stepped, 'comp', split_axis=2, concat_axis=0, tiled=True)  24.3 us
    dot_general x1, matrix products, on_device(): jnp.einsum('sk,krc->src', weights_all, fresh, precision=lax.Precision.HIG...  16.7 us
  transfers between devices with their start and end apart: 9, of which 3 were waited for; matrix products, arithmetic and copies ran while one was open for 32% of the time, Pallas kernels for 0%

commit v1 on v0

v1 whole, which is shorter than its diff:
```python
import functools

import jax
import jax.numpy as jnp
from jax import lax
from jax.experimental import pallas as pl
from jax.experimental.pallas import tpu as pltpu
from jax.sharding import PartitionSpec as P

WAVE_STEP = 0.5
SEDIMENT_STEP = 1.0
DIFFUSION = 0.2
LANES = 128
PACK = 16
CHUNK = 4
PAIR = 2


def line(count, step):
    if step > 0:
        return [(i, i + 1) for i in range(count - 1)]
    return [(i + 1, i) for i in range(count - 1)]


def wave_kernel(
    n,
    n_tile,
    x_hbm,
    coef,
    transfer_hbm,
    bins,
    weights,
    damp,
    grow,
    wind,
    wet,
    out_hbm,
    forces,
    xs,
    send,
    recv,
    table,
    whole,
    acc,
    stage,
    in_sem,
    edge_send,
    edge_recv,
    table_sem,
    out_sem,
    send_sem,
    recv_sem,
):
    me = lax.axis_index("comp")
    tile = lax.axis_index("tile")
    rows, own, width = x_hbm.shape
    cols = width // n
    full = n * own
    chunks = rows // CHUNK
    pairs = rows // PAIR
    is_top, is_bottom = tile == 0, tile == n_tile - 1
    mesh_id = pl.DeviceIdType.MESH
    above = {"tile": lax.rem(tile + n_tile - 1, n_tile)}
    below = {"tile": lax.rem(tile + 1, n_tile)}

    def load(q):
        return pltpu.make_async_copy(
            x_hbm.at[pl.ds(q * CHUNK, CHUNK)],
            xs.at[pl.ds(1 + q * CHUNK, CHUNK)],
            in_sem.at[q],
        )

    for q in range(chunks):
        load(q).start()
    get_table = pltpu.make_async_copy(transfer_hbm, table.at[pl.ds(0, full)], table_sem.at[0])
    get_table.start()

    barrier = pltpu.get_barrier_semaphore()
    for o in range(1, n):
        pl.semaphore_signal(
            barrier, inc=1, device_id={"comp": lax.rem(me + o, n)}, device_id_type=mesh_id
        )

    @pl.when(jnp.logical_not(is_bottom))
    def _():
        pl.semaphore_signal(barrier, inc=1, device_id=below, device_id_type=mesh_id)

    @pl.when(jnp.logical_not(is_top))
    def _():
        pl.semaphore_signal(barrier, inc=1, device_id=above, device_id_type=mesh_id)

    ends = is_top.astype(jnp.int32) + is_bottom.astype(jnp.int32)
    pl.semaphore_wait(barrier, n + 1 - ends)

    to_below = pltpu.make_async_remote_copy(
        src_ref=x_hbm.at[pl.ds(rows - 1, 1)],
        dst_ref=xs.at[pl.ds(0, 1)],
        send_sem=edge_send.at[0],
        recv_sem=edge_recv.at[0],
        device_id=below,
        device_id_type=mesh_id,
    )
    to_above = pltpu.make_async_remote_copy(
        src_ref=x_hbm.at[pl.ds(0, 1)],
        dst_ref=xs.at[pl.ds(rows + 1, 1)],
        send_sem=edge_send.at[1],
        recv_sem=edge_recv.at[1],
        device_id=above,
        device_id_type=mesh_id,
    )

    @pl.when(jnp.logical_not(is_bottom))
    def _():
        to_below.start()

    @pl.when(jnp.logical_not(is_top))
    def _():
        to_above.start()

    @pl.when(is_top)
    def _():
        xs[0] = jnp.zeros((own, width), jnp.bfloat16)

    @pl.when(is_bottom)
    def _():
        xs[rows + 1] = jnp.zeros((own, width), jnp.bfloat16)

    def remote(q, o, source, target):
        return pltpu.make_async_remote_copy(
            src_ref=send.at[target, pl.ds(q * CHUNK, CHUNK)],
            dst_ref=recv.at[source, pl.ds(q * CHUNK, CHUNK)],
            send_sem=send_sem.at[o - 1, q],
            recv_sem=recv_sem.at[o - 1, q],
            device_id={"comp": target},
            device_id_type=mesh_id,
        )

    blocks, rest = own // PACK, own % PACK

    def upwind(row, part, size):
        lane = lax.broadcasted_iota(jnp.int32, (size, cols), 1)
        first_lane, last_lane = lane == 0, lane == cols - 1
        kept, from_north, from_south, from_west, from_east = [coef[i, part, :] for i in range(5)]

        def tile_of(at, d):
            return xs[at, part, d * cols : (d + 1) * cols].astype(jnp.float32)

        centre = [tile_of(row + 1, d) for d in range(n)]
        right = [pltpu.roll(c, 1, 1) for c in centre]
        left = [pltpu.roll(c, cols - 1, 1) for c in centre]
        nothing = jnp.zeros((size, cols), jnp.float32)
        for d in range(n):
            west = jnp.where(first_lane, right[d - 1] if d else nothing, right[d])
            east = jnp.where(last_lane, left[d + 1] if d < n - 1 else nothing, left[d])
            moved = (
                kept * centre[d]
                + from_north * tile_of(row, d)
                + from_south * tile_of(row + 2, d)
                + from_west * west
                + from_east * east
            )
            send[d, row, part, :] = moved.astype(jnp.bfloat16)

    load(0).wait()
    load(1).wait()

    @pl.loop(0, chunks)
    def _(step):
        q = lax.rem(step + 1, chunks)

        @pl.when(step < chunks - 2)
        def _():
            load(q + 1).wait()

        @pl.when(jnp.logical_and(step == chunks - 2, jnp.logical_not(is_bottom)))
        def _():
            to_above.wait_recv()

        @pl.when(jnp.logical_and(step == chunks - 1, jnp.logical_not(is_top)))
        def _():
            to_below.wait_recv()

        @pl.loop(0, CHUNK * blocks)
        def _(i):
            start = pl.multiple_of(lax.rem(i, blocks) * PACK, PACK)
            upwind(q * CHUNK + i // blocks, pl.ds(start, PACK), PACK)

        if rest:

            @pl.loop(0, CHUNK)
            def _(i):
                upwind(q * CHUNK + i, pl.ds(blocks * PACK, rest), rest)

        for o in range(1, n):
            remote(q, o, me, lax.rem(me + o, n)).start()
        here = pl.ds(q * CHUNK, CHUNK)
        recv[me, here] = send[me, here]

    get_table.wait()
    table[full : full + PACK, :] = bins[...]

    def put(i, slot):
        return pltpu.make_async_copy(
            stage.at[slot], out_hbm.at[pl.ds(i * PAIR, PAIR)], out_sem.at[slot]
        )

    band = 3 * PACK if full % (3 * PACK) == 0 else PACK

    def mix(i, slot, is_first):
        row = i * PAIR
        for s in range(n):
            for a in range(PAIR):
                whole[s * own : (s + 1) * own, a * cols : (a + 1) * cols] = recv[
                    s, row + a
                ].astype(jnp.float32)
        acc[...] = jnp.dot(
            table[...], whole[...].astype(jnp.bfloat16), preferred_element_type=jnp.float32
        )
        total = acc[full : full + 1, :] + acc[full + 1 : full + 2, :]
        ratio = total / (total + 1.0)
        gust = jnp.concatenate([wind[pl.ds(row + a, 1), :] for a in range(PAIR)], axis=1)
        open_water = jnp.concatenate([wet[pl.ds(row + a, 1), :] for a in range(PAIR)], axis=1)

        @pl.when(jnp.logical_not(is_first))
        def _():
            put(i, slot).wait()

        @pl.loop(0, full // band)
        def _(b):
            part = pl.ds(pl.multiple_of(b * band, band), band)
            damping, growing = damp[part, :], grow[part, :]
            for a in range(PAIR):
                span = slice(a * cols, (a + 1) * cols)
                gain = 1.0 - damping * ratio[:, span] + growing * gust[:, span]
                relaxed = WAVE_STEP * acc[part, span] + whole[part, span] * gain
                fresh = open_water[:, span] * jnp.maximum(relaxed, 0.0)
                stage[slot, a, part, :] = fresh.astype(jnp.bfloat16)

        fresh_all = jnp.concatenate([stage[slot, a] for a in range(PAIR)], axis=1)
        pulled = jnp.dot(weights[...], fresh_all, preferred_element_type=jnp.float32)
        for a in range(PAIR):
            forces[row + a] = pulled[:, a * cols : (a + 1) * cols]
        put(i, slot).start()

    per_chunk = CHUNK // PAIR

    @pl.loop(0, chunks)
    def _(step):
        q = lax.rem(step + 1, chunks)
        for o in range(1, n):
            remote(q, o, lax.rem(me + n - o, n), me).wait_recv()
        for a in range(per_chunk):
            mix(q * per_chunk + a, a % 2, step == 0)

    for a in range(2):
        put(a, a).wait()

    @pl.when(jnp.logical_not(is_bottom))
    def _():
        to_below.wait_send()

    @pl.when(jnp.logical_not(is_top))
    def _():
        to_above.wait_send()

    @pl.loop(0, chunks)
    def _(q):
        for o in range(1, n):
            remote(q, o, me, lax.rem(me + o, n)).wait_send()


def split_two(values):
    high = values.astype(jnp.bfloat16)
    low = (values - high.astype(jnp.float32)).astype(jnp.bfloat16)
    return high, low


def on_device(
    spectrum,
    courant_x,
    courant_y,
    growth,
    dissipation,
    bin_width,
    transfer,
    stress_weights,
    orbital_weights,
    wind,
    wave_wet,
    owner,
    cell_index,
    current_stress,
    sediment,
    metals,
    bed_class,
    roms_wet,
    class_props,
    partition,
):
    n_comp = lax.axis_size("comp")
    n_tile = lax.axis_size("tile")
    devices = n_comp * n_tile
    own_count, rows, width = spectrum.shape
    cols = width // n_comp
    count = n_comp * own_count
    bf16, f32 = jnp.bfloat16, jnp.float32

    by_row = jnp.transpose(spectrum, (1, 0, 2))
    first = lax.axis_index("comp") * own_count
    speed_x = lax.dynamic_slice_in_dim(courant_x, first, own_count)
    speed_y = lax.dynamic_slice_in_dim(courant_y, first, own_count)
    coef = jnp.stack(
        [
            1.0 - jnp.abs(speed_x) - jnp.abs(speed_y),
            jnp.maximum(speed_x, 0.0),
            -jnp.minimum(speed_x, 0.0),
            jnp.maximum(speed_y, 0.0),
            -jnp.minimum(speed_y, 0.0),
        ]
    )
    coef = jnp.broadcast_to(coef[:, :, None], (5, own_count, cols))
    bins = jnp.pad(jnp.stack(split_two(bin_width)), ((0, PACK - 2), (0, 0)))
    weights_all = jnp.concatenate([stress_weights, orbital_weights[None, :]], axis=0)
    weights = jnp.pad(jnp.concatenate(split_two(weights_all), axis=0), ((0, PACK - 6), (0, 0)))
    damp = jnp.broadcast_to((WAVE_STEP * dissipation)[:, None], (count, cols))
    grow = jnp.broadcast_to((WAVE_STEP * growth)[:, None], (count, cols))

    vmem = pl.BlockSpec(memory_space=pltpu.VMEM)
    hbm = pl.BlockSpec(memory_space=pl.ANY)
    chunks = rows // CHUNK
    fresh, pulled = pl.pallas_call(
        functools.partial(wave_kernel, n_comp, n_tile),
        out_shape=(
            jax.ShapeDtypeStruct((rows, count, cols), bf16),
            jax.ShapeDtypeStruct((rows, PACK, cols), f32),
        ),
        in_specs=[hbm, vmem, hbm] + [vmem] * 6,
        out_specs=(hbm, vmem),
        scratch_shapes=[
            pltpu.VMEM((rows + 2, own_count, width), bf16),
            pltpu.VMEM((n_comp, rows, own_count, cols), bf16),
            pltpu.VMEM((n_comp, rows, own_count, cols), bf16),
            pltpu.VMEM((count + PACK, count), bf16),
            pltpu.VMEM((count, PAIR * cols), f32),
            pltpu.VMEM((count + PACK, PAIR * cols), f32),
            pltpu.VMEM((2, PAIR, count, cols), bf16),
            pltpu.SemaphoreType.DMA((chunks,)),
            pltpu.SemaphoreType.DMA((2,)),
            pltpu.SemaphoreType.DMA((2,)),
            pltpu.SemaphoreType.DMA((1,)),
            pltpu.SemaphoreType.DMA((2,)),
            pltpu.SemaphoreType.DMA((n_comp - 1, chunks)),
            pltpu.SemaphoreType.DMA((n_comp - 1, chunks)),
        ],
        compiler_params=pltpu.CompilerParams(
            collective_id=0, has_side_effects=True, vmem_limit_bytes=63000 * 1024
        ),
    )(by_row, coef, transfer, bins, weights, damp, grow, wind, wave_wet.astype(f32))
    spectrum_new = jnp.transpose(fresh, (1, 0, 2))
    forces = pulled[:, :3] + pulled[:, 3:6]

    points = rows * cols
    slots = max(2, 3 * points // devices)
    cells_r, cells_c = sediment.shape[1], sediment.shape[2]
    owner_rc = owner.reshape(rows, cols)
    cell_rc = cell_index.reshape(rows, cols)
    hit = owner_rc[None] == jnp.arange(devices, dtype=jnp.int32)[:, None, None]
    hits = hit.astype(bf16)
    before_col = (jnp.arange(cols)[:, None] < jnp.arange(cols)[None, :]).astype(bf16)
    before_row = (jnp.arange(rows)[:, None] < jnp.arange(rows)[None, :]).astype(bf16)
    in_row = jnp.einsum("orc,cd->ord", hits, before_col, preferred_element_type=f32)
    row_sum = jnp.sum(hits.astype(f32), axis=2).astype(bf16)
    above = jnp.einsum("or,rs->os", row_sum, before_row, preferred_element_type=f32)
    rank = jnp.sum(jnp.where(hit, in_row + above[:, :, None], 0.0), axis=0).reshape(points)
    placed = (
        rank.astype(jnp.int32)[None, :] == jnp.arange(slots, dtype=jnp.int32)[:, None]
    ).astype(bf16)
    items = jnp.concatenate(
        [
            jnp.transpose(forces, (1, 0, 2)).astype(bf16),
            (cell_rc // cells_c).astype(bf16)[None],
            (cell_rc % cells_c).astype(bf16)[None],
        ],
        axis=0,
    ).reshape(5, 1, points)
    spreaded = (items * hits.reshape(1, devices, points)).reshape(5 * devices, points)
    packed = lax.dot_general(
        spreaded, placed, (((1,), (1,)), ((), ())), preferred_element_type=f32
    ).astype(bf16)
    got = lax.all_to_all(
        packed.reshape(5, devices, slots), ("comp", "tile"), split_axis=1, concat_axis=1, tiled=True
    ).reshape(5, devices * slots)
    at_row = got[3][None, :] == jnp.arange(cells_r, dtype=jnp.int32).astype(bf16)[:, None]
    at_col = got[4][None, :] == jnp.arange(cells_c, dtype=jnp.int32).astype(bf16)[:, None]
    lifted = jnp.where(at_row[None], got[:3, None, :], jnp.zeros((), bf16))
    bottom = lax.dot_general(
        lifted.reshape(3 * cells_r, devices * slots),
        at_col.astype(bf16),
        (((1,), (1,)), ((), ())),
        preferred_element_type=f32,
    ).reshape(3, cells_r, cells_c)

    shear_x = current_stress[0] + bottom[0]
    shear_y = current_stress[1] + bottom[1]
    shear = jnp.sqrt(shear_x * shear_x + shear_y * shear_y + bottom[2])
    classes_count = sediment.shape[0]
    low_share = 0.5 / classes_count
    high_share = 1.0 - (classes_count - 1) * low_share
    classes = jnp.arange(classes_count, dtype=jnp.int32)[:, None, None]
    fraction = jnp.where(bed_class[None] == classes, high_share, low_share)
    erosion = (
        class_props[0][:, None, None]
        * fraction
        * jnp.maximum(shear[None] / class_props[1][:, None, None] - 1.0, 0.0)
    )
    wetness = roms_wet.astype(f32)
    settled = wetness * (
        sediment + SEDIMENT_STEP * (erosion - class_props[2][:, None, None] * sediment)
    )
    carried = wetness * metals
    fields = jnp.concatenate([settled, carried], axis=0)
    from_north = lax.ppermute(fields[:, -1:, :], "tile", line(n_tile, 1))
    from_south = lax.ppermute(fields[:, :1, :], "tile", line(n_tile, -1))
    from_west = lax.ppermute(fields[:, :, -1:], "comp", line(n_comp, 1))
    from_east = lax.ppermute(fields[:, :, :1], "comp", line(n_comp, -1))
    tall = jnp.concatenate([from_north, fields, from_south], axis=1)
    wide = jnp.concatenate([from_west, fields, from_east], axis=2)
    beside_all = tall[:, :-2] + tall[:, 2:] + wide[:, :, :-2] + wide[:, :, 2:]
    diffused = wetness * (fields + DIFFUSION * (beside_all - 4.0 * fields))
    sediment_new = diffused[:classes_count]
    spread_new = diffused[classes_count:]
    denominator = 1.0 + jnp.sum(partition[:, :, None, None] * sediment_new[None], axis=1)
    dissolved = spread_new / denominator
    sorbed = spread_new - dissolved
    return (spectrum_new, sediment_new, dissolved, sorbed)


def solution(mesh):
    in_specs = (
        P("comp", "tile", None),
        P(),
        P(),
        P(),
        P(),
        P(),
        P(),
        P(),
        P(),
        P("tile", "comp"),
        P("tile", "comp"),
        P("tile", "comp", None, None, None),
        P("tile", "comp", None, None),
        P(None, "tile", "comp"),
        P(None, "tile", "comp"),
        P(None, "tile", "comp"),
        P("tile", "comp"),
        P("tile", "comp"),
        P(),
        P(),
    )
    out_specs = (
        P(None, "tile", "comp"),
        P(None, "tile", "comp"),
        P(None, "tile", "comp"),
        P(None, "tile", "comp"),
    )
    return jax.shard_map(
        on_device, mesh=mesh, in_specs=in_specs, out_specs=out_specs, check_vma=False
    )
```

time: 559 us -> 209 us (0.37); the launches traced: 549 us -> 208 us
  other arithmetic: 178 us -> 7.32 us
  waiting for transfers between devices: 165 us -> 7.09 us
  Pallas kernels: 0 us -> 137 us
  local copies, waits for them, and re-layouts: 111 us -> 35 us
  matrix products: 59.6 us -> 3.15 us
  starting transfers between devices: 34.2 us -> 16.6 us
    all_to_all x3 -> x1, waiting for transfers between devices: 161 us -> 7.08 us  [on_device(): lax.all_to_all(packed.reshape(5, devices, slots), ('comp', 'tile'), split...]
    pallas_call x0 -> x1, Pallas kernels: none -> 137 us  [on_device(): pl.pallas_call(functools.partial(wave_kernel, n_comp, n_tile), out_shape=...]
    convert_element_type x6 -> x11, other arithmetic: 99.3 us -> 3.02 us  [the longest x2 1.5 us: split_two(): low = (values - high.astype(jnp.float32)).astype(jnp.bfloat16)]
    scatter-add x1 -> x0, other arithmetic: 66.2 us -> none  [on_device(): bottom = jnp.zeros((3, cells), jnp.float32).at[:, got_labels.reshape(-1)]...]
    dot_general x4, matrix products: 59.6 us -> 3.15 us  [the longest x1 1.39 us: on_device(): lax.dot_general(lifted.reshape(3 * cells_r, devices * slots), at_col.asty...]
    scatter x2 -> x0, local copies, waits for them, and re-layouts: 30 us -> none  [the longest x1 16.3 us: on_device(): jnp.full((devices * slots,), cells, jnp.int32).at[target].set(cell_flat)]
    all_to_all x1 -> x0, local copies, waits for them, and re-layouts: 24.3 us -> none  [on_device(): lax.all_to_all(stepped, 'comp', split_axis=2, concat_axis=0, tiled=True)]
    all_to_all x3 -> x1, starting transfers between devices: 18.5 us -> 5.32 us  [on_device(): lax.all_to_all(packed.reshape(5, devices, slots), ('comp', 'tile'), split...]
  transfers between devices with their start and end apart: 9 -> 5, of which waited for: 3 -> 1; matrix products, arithmetic and copies ran while one was open for 32% -> 8% of each run, Pallas kernels for 0% -> 0%
where the time goes in v1:
time: 209 us; the launch traced here: 208 us
  Pallas kernels  137 us (66%)
  local copies, waits for them, and re-layouts  35 us (17%)
  starting transfers between devices  16.6 us (8%)
  other arithmetic  7.32 us (4%)
  waiting for transfers between devices  7.09 us (3%)
  matrix products  3.15 us (2%)
    pallas_call x1, Pallas kernels, on_device(): pl.pallas_call(functools.partial(wave_kernel, n_comp, n_tile), out_shape=...  137 us
    unnamed x28, local copies, waits for them, and re-layouts  30 us
    all_to_all x1, waiting for transfers between devices, on_device(): lax.all_to_all(packed.reshape(5, devices, slots), ('comp', 'tile'), split...  7.08 us
    all_to_all x1, starting transfers between devices, on_device(): lax.all_to_all(packed.reshape(5, devices, slots), ('comp', 'tile'), split...  5.32 us
  transfers between devices with their start and end apart: 5, of which 1 were waited for; matrix products, arithmetic and copies ran while one was open for 8% of the time, Pallas kernels for 0%

profile of v1, /device:TPU:11, one launch (start us, length us, event | category | flops | bytes accessed | tf_op | source)
XLA Modules:
  0.0 207.5 jit_solution(5542040583298289643)
XLA Ops:
  0.6 0.7 broadcast_in_dim.34
  1.3 0.7 fusion.36
  2.1 0.7 subtract_convert_fusion
  2.8 0.8 subtract_convert_fusion.1
  3.6 0.0 copy-start.8
  3.6 0.0 copy-start.9
  3.6 0.0 copy-start.6
  3.6 13.1 %copy.38 = bf16[162,32,1024]{2,0,1:T(8,128)(2,1)} copy(bf16[162,32,1024]{2,1,0:T(8,128)(2,1)} %param.20) | data formatting | bytes 21233664 | tf_op args[0]
  16.8 0.0 copy-done.8
  16.8 0.0 copy-done.9
  16.8 0.0 copy-done.6
  16.8 0.6 convert_element_type.104.wet
  17.4 0.8 minimum_negate_fusion
  18.2 0.7 fusion.28
  18.9 0.9 broadcast_in_dim.33.coef
  19.8 1.1 broadcast_in_dim.35.damp
  20.9 1.1 broadcast_in_dim.43.grow
  22.0 137.4 %shard_map.219 = (bf16[32,1296,128]{2,1,0:T(8,128)(2,1)}, f32[32,16,128]{2,1,0:T(8,128)}) custom-call(bf16[32,162,1024]{2,1,0:T(8,128)(2,1)} %bitcast.64, f32[5,162,128]{2,1,0:T(8,128)} %broadcast_in_dim.33.coef, bf16[1296,1296]{1,0:T(8,128)(2,1)} %transfer_hbm.1, bf16[16,1296]{1,0:T(8,128)(2,1)} %get-tuple-element.50.bins, ...), custom_call_target="tpu_custom_call" | custom-call | tf_op jit(solution)/shard_map/pallas_call | solution.py:331
  159.4 1.0 fusion.35
  160.4 0.0 copy-done.4
  160.4 0.1 fusion.39
  160.5 0.0 copy-done.1
  160.6 0.2 fusion.11
  160.8 0.1 fusion.38
  160.9 0.3 fusion.7
  161.2 0.1 maximum_bitcast_fusion
  161.3 0.1 broadcast_multiply_fusion
  161.4 0.0 copy-start.10
  161.4 0.0 copy-start.12
  161.4 1.4 fusion.8
  162.8 0.7 copy.35
  163.5 5.3 %all-to-all-start = ((bf16[5,32,384]{2,0,1:T(8,128)(2,1)}), bf16[5,32,384]{2,0,1:T(8,128)(2,1)S(1)}, u32[]{:S(2)}, u32[]{:S(2)}) async-start(bf16[5,32,384]{2,0,1:T(8,128)(2,1)} %copy.35), calls=%async_computation | async-start | bytes 393216 | tf_op jit(solution)/shard_map/all_to_all | solution.py:390
  168.9 0.0 copy-done.10
  168.9 0.0 copy-done.12
  168.9 7.1 %all-to-all-done = bf16[5,32,384]{2,0,1:T(8,128)(2,1)S(1)} async-done(((bf16[5,32,384]{2,0,1:T(8,128)(2,1)}), bf16[5,32,384]{2,0,1:T(8,128)(2,1)S(1)}, u32[]{:S(2)}, u32[]{:S(2)}) %all-to-all-start) | async-done | bytes 122912 | tf_op jit(solution)/shard_map/all_to_all | solution.py:390
  176.0 0.3 slice_reduce_fusion
  176.4 0.2 broadcast_compare_fusion
  176.6 0.2 broadcast_select_fusion
  176.8 0.0 copy-start.5
  176.8 0.0 copy-start.2
  176.8 0.0 copy-start.3
  176.8 0.0 copy-start.7
  176.8 1.4 fusion.1
  178.2 0.0 copy-done.5
  178.3 0.0 copy-done.2
  178.3 0.0 copy-done.3
  178.3 0.0 copy-done.7
  178.3 0.1 broadcast_multiply_fusion.1
  178.4 2.5 %collective-permute-start = (f32[8,1,128]{2,1,0:T(1,128)S(1)}, f32[8,1,128]{2,1,0:T(1,128)S(1)}, u32[]{:S(2)}, u32[]{:S(2)}) collective-permute-start(f32[8,1,128]{2,1,0:T(1,128)S(1)} %get-tuple-element.36), channel_id=1, source_target_pairs={{0,1},{1,2},{2,3},{4,5},{5,6},{6,7},{8,9},{9,10},{10,11},{12,13},{... | collective-permute-start | bytes 12296 | tf_op jit(solution)/shard_map/ppermute | solution.py:422
  180.9 2.8 %collective-permute-start.1 = (f32[8,1,128]{2,1,0:T(1,128)S(1)}, f32[8,1,128]{2,1,0:T(1,128)S(1)}, u32[]{:S(2)}, u32[]{:S(2)}) collective-permute-start(f32[8,1,128]{2,1,0:T(1,128)S(1)} %get-tuple-element.37), channel_id=1, source_target_pairs={{1,0},{2,1},{3,2},{5,4},{6,5},{7,6},{9,8},{10,9},{11,10},{13,12},{... | collective-permute-start | bytes 12296 | tf_op jit(solution)/shard_map/ppermute | solution.py:423
  183.7 0.1 fusion.17
  183.8 3.9 %collective-permute-start.2 = (f32[8,16,1]{2,1,0:T(8,128)S(1)}, f32[8,16,1]{2,1,0:T(8,128)S(1)}, u32[]{:S(2)}, u32[]{:S(2)}) collective-permute-start(f32[8,16,1]{2,1,0:T(8,128)S(1)} %get-tuple-element.38), channel_id=1, source_target_pairs={{0,4},{4,8},{8,12},{12,16},{16,20},{20,24},{24,28},{1,5},{5,9},{9,... | collective-permute-start | bytes 1544 | tf_op jit(solution)/shard_map/ppermute | solution.py:424
  187.7 2.1 %collective-permute-start.3 = (f32[8,16,1]{2,1,0:T(8,128)S(1)}, f32[8,16,1]{2,1,0:T(8,128)S(1)}, u32[]{:S(2)}, u32[]{:S(2)}) collective-permute-start(f32[8,16,1]{2,1,0:T(8,128)S(1)} %get-tuple-element.39), channel_id=1, source_target_pairs={{4,0},{8,4},{12,8},{16,12},{20,16},{24,20},{28,24},{5,1},{9,5},{13... | collective-permute-start | bytes 1544 | tf_op jit(solution)/shard_map/ppermute | solution.py:425
  189.8 0.0 copy-start.11
  189.8 16.8 %copy.36 = bf16[1296,32,128]{2,1,0:T(8,128)(2,1)} copy(bf16[1296,32,128]{2,0,1:T(8,128)(2,1)} %bitcast.65) | data formatting | bytes 21233664
  206.6 0.0 collective-permute-done.2
  206.6 0.0 collective-permute-done.3
  206.6 0.0 collective-permute-done
  206.6 0.0 collective-permute-done.1
  206.6 0.1 fusion.23
  206.7 0.0 copy-done.11
  206.8 0.0 copy-start
  206.8 0.1 multiply_reduce_fusion
  206.9 0.6 slice_subtract_fusion
  (21 shorter events, 0.3 us)
Async XLA Ops:
  3.6 13.2 %copy-start.8 = (f32[1296]{0:T(1024)S(1)}, f32[1296]{0:T(1024)}, u32[]{:S(2)}) copy-start(f32[1296]{0:T(1024)} %param.24) | copy-start | bytes 15556
  3.6 13.2 %copy-start.9 = (f32[1296]{0:T(1024)S(1)}, f32[1296]{0:T(1024)}, u32[]{:S(2)}) copy-start(f32[1296]{0:T(1024)} %param.23) | copy-start | bytes 15556
  3.6 13.2 %copy-start.6 = (s32[32,128]{1,0:T(8,128)S(1)}, s32[32,128]{1,0:T(8,128)}, u32[]{:S(2)}) copy-start(s32[32,128]{1,0:T(8,128)} %param.30) | copy-start | bytes 49156
  22.0 138.4 %copy-start.4 = (s32[1,1,32,128]{3,2,1,0:T(8,128)S(1)}, s32[1,1,32,128]{3,2,1,0:T(8,128)}, u32[]{:S(2)}) copy-start(s32[1,1,32,128]{3,2,1,0:T(8,128)} %param.32) | copy-start | bytes 49156
  22.0 138.5 %copy-start.1 = (s32[1,1,32,128,1]{3,4,2,1,0:T(1,128)S(1)}, s32[1,1,32,128,1]{3,4,2,1,0:T(1,128)}, u32[]{:S(2)}) copy-start(s32[1,1,32,128,1]{3,4,2,1,0:T(1,128)} %param.31) | copy-start | bytes 49156
  161.4 7.5 %copy-start.10 = (s32[16,128]{1,0:T(8,128)S(1)}, s32[16,128]{1,0:T(8,128)}, u32[]{:S(2)}) copy-start(s32[16,128]{1,0:T(8,128)} %param.37) | copy-start | bytes 24580
  161.4 7.5 %copy-start.12 = (f32[3,4]{1,0:T(4,128)S(1)}, f32[3,4]{1,0:T(4,128)}, u32[]{:S(2)}) copy-start(f32[3,4]{1,0:T(4,128)} %param.38) | copy-start | bytes 148
  163.5 12.5 %all-to-all-start = ((bf16[5,32,384]{2,0,1:T(8,128)(2,1)}), bf16[5,32,384]{2,0,1:T(8,128)(2,1)S(1)}, u32[]{:S(2)}, u32[]{:S(2)}) async-start(bf16[5,32,384]{2,0,1:T(8,128)(2,1)} %copy.35), calls=%async_computation | async-start | bytes 393216 | tf_op jit(solution)/shard_map/all_to_all | solution.py:390
  176.8 1.4 copy-start.5
  176.8 1.5 copy-start.2
  176.8 1.5 copy-start.3
  176.8 1.5 copy-start.7
  178.4 28.2 %collective-permute-start = (f32[8,1,128]{2,1,0:T(1,128)S(1)}, f32[8,1,128]{2,1,0:T(1,128)S(1)}, u32[]{:S(2)}, u32[]{:S(2)}) collective-permute-start(f32[8,1,128]{2,1,0:T(1,128)S(1)} %get-tuple-element.36), channel_id=1, source_target_pairs={{0,1},{1,2},{2,3},{4,5},{5,6},{6,7},{8,9},{9,10},{10,11},{12,13},{... | collective-permute-start | bytes 12296 | tf_op jit(solution)/shard_map/ppermute | solution.py:422
  180.9 25.7 %collective-permute-start.1 = (f32[8,1,128]{2,1,0:T(1,128)S(1)}, f32[8,1,128]{2,1,0:T(1,128)S(1)}, u32[]{:S(2)}, u32[]{:S(2)}) collective-permute-start(f32[8,1,128]{2,1,0:T(1,128)S(1)} %get-tuple-element.37), channel_id=1, source_target_pairs={{1,0},{2,1},{3,2},{5,4},{6,5},{7,6},{9,8},{10,9},{11,10},{13,12},{... | collective-permute-start | bytes 12296 | tf_op jit(solution)/shard_map/ppermute | solution.py:423
  183.8 22.8 %collective-permute-start.2 = (f32[8,16,1]{2,1,0:T(8,128)S(1)}, f32[8,16,1]{2,1,0:T(8,128)S(1)}, u32[]{:S(2)}, u32[]{:S(2)}) collective-permute-start(f32[8,16,1]{2,1,0:T(8,128)S(1)} %get-tuple-element.38), channel_id=1, source_target_pairs={{0,4},{4,8},{8,12},{12,16},{16,20},{20,24},{24,28},{1,5},{5,9},{9,... | collective-permute-start | bytes 1544 | tf_op jit(solution)/shard_map/ppermute | solution.py:424
  187.7 18.9 %collective-permute-start.3 = (f32[8,16,1]{2,1,0:T(8,128)S(1)}, f32[8,16,1]{2,1,0:T(8,128)S(1)}, u32[]{:S(2)}, u32[]{:S(2)}) collective-permute-start(f32[8,16,1]{2,1,0:T(8,128)S(1)} %get-tuple-element.39), channel_id=1, source_target_pairs={{4,0},{8,4},{12,8},{16,12},{20,16},{24,20},{28,24},{5,1},{9,5},{13... | collective-permute-start | bytes 1544 | tf_op jit(solution)/shard_map/ppermute | solution.py:425
  189.8 17.0 %copy-start.11 = (f32[4,4]{1,0:T(4,128)S(1)}, f32[4,4]{1,0:T(4,128)}, u32[]{:S(2)}) copy-start(f32[4,4]{1,0:T(4,128)} %param.39) | copy-start | bytes 196
  206.8 0.7 copy-start

commit v2 on v1

--- a/solution.py
+++ b/solution.py
@@ -269,6 +269,29 @@
             remote(q, o, me, lax.rem(me + o, n)).wait_send()
 
 
+def reorder_kernel(x, out, held):
+    rows, band, cols = x.shape
+    for i in range(rows):
+        held[pl.ds(i, band, stride=rows), :] = x[i].astype(jnp.float32)
+    out[...] = held[...].reshape(band, rows, cols).astype(jnp.bfloat16)
+
+
+def reorder(fresh):
+    rows, count, cols = fresh.shape
+    band = 3 * PACK if count % (3 * PACK) == 0 else PACK
+    return pl.pallas_call(
+        reorder_kernel,
+        out_shape=jax.ShapeDtypeStruct((count, rows, cols), jnp.bfloat16),
+        grid=(count // band,),
+        in_specs=[pl.BlockSpec((rows, band, cols), lambda i: (0, i, 0))],
+        out_specs=pl.BlockSpec((band, rows, cols), lambda i: (i, 0, 0)),
+        scratch_shapes=[pltpu.VMEM((band * rows, cols), jnp.float32)],
+        cost_estimate=pl.CostEstimate(
+            flops=fresh.size, bytes_accessed=4 * fresh.size, transcendentals=0
+        ),
+    )(fresh)
+
+
 def split_two(values):
     high = values.astype(jnp.bfloat16)
     low = (values - high.astype(jnp.float32)).astype(jnp.bfloat16)
@@ -356,7 +379,7 @@
             collective_id=0, has_side_effects=True, vmem_limit_bytes=63000 * 1024
         ),
     )(by_row, coef, transfer, bins, weights, damp, grow, wind, wave_wet.astype(f32))
-    spectrum_new = jnp.transpose(fresh, (1, 0, 2))
+    spectrum_new = reorder(fresh)
     forces = pulled[:, :3] + pulled[:, 3:6]
 
     points = rows * cols
@@ -389,7 +412,9 @@
     ).astype(bf16)
     got = lax.all_to_all(
         packed.reshape(5, devices, slots), ("comp", "tile"), split_axis=1, concat_axis=1, tiled=True
-    ).reshape(5, devices * slots)
+    )
+    got, spectrum_new = lax.optimization_barrier((got, spectrum_new))
+    got = got.reshape(5, devices * slots)
     at_row = got[3][None, :] == jnp.arange(cells_r, dtype=jnp.int32).astype(bf16)[:, None]
     at_col = got[4][None, :] == jnp.arange(cells_c, dtype=jnp.int32).astype(bf16)[:, None]
     lifted = jnp.where(at_row[None], got[:3, None, :], jnp.zeros((), bf16))

time: 209 us -> 218 us (1.043)
  Pallas kernels: 137 us -> 166 us
  local copies, waits for them, and re-layouts: 35 us -> 18.2 us
  waiting for transfers between devices: 7.09 us -> 4.56 us
    pallas_call x0 -> x1, Pallas kernels: none -> 28.2 us  [reorder(): pl.pallas_call(reorder_kernel, out_shape=jax.ShapeDtypeStruct((count, row...]
    unnamed x28 -> x27, local copies, waits for them, and re-layouts: 30 us -> 13.2 us
    all_to_all x1, waiting for transfers between devices: 7.08 us -> 0.01 us  [on_device(): lax.all_to_all(packed.reshape(5, devices, slots), ('comp', 'tile'), split...]
    ppermute x1, waiting for transfers between devices: 0.01 us -> 4.54 us  [on_device(): from_east = lax.ppermute(fields[:, :, :1], 'comp', line(n_comp, -1))]
  transfers between devices with their start and end apart: 5 -> 5, of which waited for: 1 -> 1; matrix products, arithmetic and copies ran while one was open for 8% -> 0% of each run, Pallas kernels for 0% -> 13%
where the time goes in v2:
time: 218 us; the launch traced here: 216 us
  Pallas kernels  166 us (76%)
  local copies, waits for them, and re-layouts  18.2 us (8%)
  starting transfers between devices  16.4 us (8%)
  other arithmetic  7.31 us (3%)
  waiting for transfers between devices  4.56 us (2%)
  matrix products  3.15 us (1%)
    pallas_call x1, Pallas kernels, on_device(): pl.pallas_call(functools.partial(wave_kernel, n_comp, n_tile), out_shape=...  137 us
    pallas_call x1, Pallas kernels, reorder(): pl.pallas_call(reorder_kernel, out_shape=jax.ShapeDtypeStruct((count, row...  28.2 us
    unnamed x27, local copies, waits for them, and re-layouts  13.2 us
    all_to_all x1, starting transfers between devices, on_device(): lax.all_to_all(packed.reshape(5, devices, slots), ('comp', 'tile'), split...  5.32 us
    ppermute x1, waiting for transfers between devices, on_device(): from_east = lax.ppermute(fields[:, :, :1], 'comp', line(n_comp, -1))  4.54 us
  transfers between devices with their start and end apart: 5, of which 1 were waited for; matrix products, arithmetic and copies ran while one was open for 0% of the time, Pallas kernels for 13%

profile of v2, /device:TPU:11, one launch (start us, length us, event | category | flops | bytes accessed | tf_op | source)
XLA Modules:
  0.0 216.2 jit_solution(5342984337306433303)
XLA Ops:
  0.6 0.7 broadcast_in_dim.34
  1.3 0.7 fusion.36
  2.1 0.7 subtract_convert_fusion
  2.8 0.8 subtract_convert_fusion.1
  3.6 0.0 copy-start.8
  3.6 0.0 copy-start.9
  3.6 0.0 copy-start.6
  3.6 13.1 %copy.33 = bf16[162,32,1024]{2,0,1:T(8,128)(2,1)} copy(bf16[162,32,1024]{2,1,0:T(8,128)(2,1)} %param.20) | data formatting | bytes 21233664 | tf_op args[0]
  16.8 0.0 copy-done.8
  16.8 0.0 copy-done.9
  16.8 0.0 copy-done.6
  16.8 0.6 convert_element_type.104.wet
  17.4 0.8 minimum_negate_fusion
  18.2 0.7 fusion.28
  18.9 0.9 broadcast_in_dim.33.coef
  19.8 1.1 broadcast_in_dim.35.damp
  20.9 1.1 broadcast_in_dim.43.grow
  22.0 137.4 %shard_map.219 = (bf16[32,1296,128]{2,1,0:T(8,128)(2,1)}, f32[32,16,128]{2,1,0:T(8,128)}) custom-call(bf16[32,162,1024]{2,1,0:T(8,128)(2,1)} %bitcast.63, f32[5,162,128]{2,1,0:T(8,128)} %broadcast_in_dim.33.coef, bf16[1296,1296]{1,0:T(8,128)(2,1)} %transfer_hbm.1, bf16[16,1296]{1,0:T(8,128)(2,1)} %get-tuple-element.34.bins, ...), custom_call_target="tpu_custom_call" | custom-call | tf_op jit(solution)/shard_map/pallas_call | solution.py:354
  159.4 1.0 fusion.35
  160.4 0.0 copy-done.4
  160.4 0.1 fusion.39
  160.5 0.0 copy-done.1
  160.6 0.2 fusion.11
  160.8 0.1 fusion.38
  160.9 0.3 fusion.7
  161.2 0.1 maximum_bitcast_fusion
  161.3 0.1 broadcast_multiply_fusion
  161.4 0.0 copy-start.10
  161.4 1.4 fusion.8
  162.8 0.7 copy.31
  163.5 5.3 %all-to-all-start = ((bf16[5,32,384]{2,0,1:T(8,128)(2,1)}), bf16[5,32,384]{2,0,1:T(8,128)(2,1)S(1)}, u32[]{:S(2)}, u32[]{:S(2)}) async-start(bf16[5,32,384]{2,0,1:T(8,128)(2,1)} %copy.31), calls=%async_computation | async-start | bytes 393216 | tf_op jit(solution)/shard_map/all_to_all | solution.py:413
  168.9 0.0 copy-done.10
  168.9 0.0 copy-start.12
  168.9 28.2 %shard_map.220 = bf16[1296,32,128]{2,1,0:T(8,128)(2,1)} custom-call(bf16[32,1296,128]{2,1,0:T(8,128)(2,1)} %get-tuple-element.9.x), custom_call_target="tpu_custom_call" | custom-call | flops 5308416 | bytes 21233664 | tf_op jit(solution)/shard_map/pallas_call | solution.py:282
  197.1 0.0 copy-done.12
  197.1 0.0 all-to-all-done
  197.1 0.3 slice_reduce_fusion
  197.5 0.2 broadcast_compare_fusion
  197.7 0.2 broadcast_select_fusion
  197.9 0.0 copy-start.5
  197.9 0.0 copy-start.2
  197.9 0.0 copy-start.3
  198.0 0.0 copy-start.7
  198.0 0.0 copy-start.11
  198.0 1.4 fusion.1
  199.4 0.0 copy-done.2
  199.4 0.0 copy-done.3
  199.4 0.0 copy-done.7
  199.4 0.1 broadcast_multiply_fusion.1
  199.5 3.1 %collective-permute-start = (f32[8,1,128]{2,1,0:T(1,128)S(1)}, f32[8,1,128]{2,1,0:T(1,128)S(1)}, u32[]{:S(2)}, u32[]{:S(2)}) collective-permute-start(f32[8,1,128]{2,1,0:T(1,128)S(1)} %get-tuple-element.20), channel_id=1, source_target_pairs={{0,1},{1,2},{2,3},{4,5},{5,6},{6,7},{8,9},{9,10},{10,11},{12,13},{... | collective-permute-start | bytes 12296 | tf_op jit(solution)/shard_map/ppermute | solution.py:447
  202.7 2.2 %collective-permute-start.1 = (f32[8,1,128]{2,1,0:T(1,128)S(1)}, f32[8,1,128]{2,1,0:T(1,128)S(1)}, u32[]{:S(2)}, u32[]{:S(2)}) collective-permute-start(f32[8,1,128]{2,1,0:T(1,128)S(1)} %get-tuple-element.21), channel_id=1, source_target_pairs={{1,0},{2,1},{3,2},{5,4},{6,5},{7,6},{9,8},{10,9},{11,10},{13,12},{... | collective-permute-start | bytes 12296 | tf_op jit(solution)/shard_map/ppermute | solution.py:448
  204.8 0.1 fusion.17
  204.9 3.9 %collective-permute-start.2 = (f32[8,16,1]{2,1,0:T(8,128)S(1)}, f32[8,16,1]{2,1,0:T(8,128)S(1)}, u32[]{:S(2)}, u32[]{:S(2)}) collective-permute-start(f32[8,16,1]{2,1,0:T(8,128)S(1)} %get-tuple-element.22), channel_id=1, source_target_pairs={{0,4},{4,8},{8,12},{12,16},{16,20},{20,24},{24,28},{1,5},{5,9},{9,... | collective-permute-start | bytes 1544 | tf_op jit(solution)/shard_map/ppermute | solution.py:449
  208.9 1.9 collective-permute-start.3
  210.8 0.0 collective-permute-done.2
  210.8 4.5 %collective-permute-done.3 = f32[8,16,1]{2,1,0:T(8,128)S(1)} collective-permute-done((f32[8,16,1]{2,1,0:T(8,128)S(1)}, f32[8,16,1]{2,1,0:T(8,128)S(1)}, u32[]{:S(2)}, u32[]{:S(2)}) %collective-permute-start.3) | collective-permute-done | bytes 544 | tf_op jit(solution)/shard_map/ppermute | solution.py:450
  215.3 0.0 collective-permute-done
  215.3 0.0 collective-permute-done.1
  215.3 0.1 fusion.23
  215.5 0.0 copy-done.11
  215.5 0.0 copy-start
  215.5 0.1 multiply_reduce_fusion
  215.6 0.6 slice_subtract_fusion
  216.2 0.0 copy-done
  (21 shorter events, 0.3 us)
Async XLA Ops:
  3.6 13.2 %copy-start.8 = (f32[1296]{0:T(1024)S(1)}, f32[1296]{0:T(1024)}, u32[]{:S(2)}) copy-start(f32[1296]{0:T(1024)} %param.24) | copy-start | bytes 15556
  3.6 13.2 %copy-start.9 = (f32[1296]{0:T(1024)S(1)}, f32[1296]{0:T(1024)}, u32[]{:S(2)}) copy-start(f32[1296]{0:T(1024)} %param.23) | copy-start | bytes 15556
  3.6 13.2 %copy-start.6 = (s32[32,128]{1,0:T(8,128)S(1)}, s32[32,128]{1,0:T(8,128)}, u32[]{:S(2)}) copy-start(s32[32,128]{1,0:T(8,128)} %param.30) | copy-start | bytes 49156
  22.0 138.4 %copy-start.4 = (s32[1,1,32,128]{3,2,1,0:T(8,128)S(1)}, s32[1,1,32,128]{3,2,1,0:T(8,128)}, u32[]{:S(2)}) copy-start(s32[1,1,32,128]{3,2,1,0:T(8,128)} %param.32) | copy-start | bytes 49156
  22.0 138.5 %copy-start.1 = (s32[1,1,32,128,1]{3,4,2,1,0:T(1,128)S(1)}, s32[1,1,32,128,1]{3,4,2,1,0:T(1,128)}, u32[]{:S(2)}) copy-start(s32[1,1,32,128,1]{3,4,2,1,0:T(1,128)} %param.31) | copy-start | bytes 49156
  161.4 7.5 %copy-start.10 = (s32[16,128]{1,0:T(8,128)S(1)}, s32[16,128]{1,0:T(8,128)}, u32[]{:S(2)}) copy-start(s32[16,128]{1,0:T(8,128)} %param.37) | copy-start | bytes 24580
  163.5 33.6 %all-to-all-start = ((bf16[5,32,384]{2,0,1:T(8,128)(2,1)}), bf16[5,32,384]{2,0,1:T(8,128)(2,1)S(1)}, u32[]{:S(2)}, u32[]{:S(2)}) async-start(bf16[5,32,384]{2,0,1:T(8,128)(2,1)} %copy.31), calls=%async_computation | async-start | bytes 393216 | tf_op jit(solution)/shard_map/all_to_all | solution.py:413
  168.9 28.2 %copy-start.12 = (f32[3,4]{1,0:T(4,128)S(1)}, f32[3,4]{1,0:T(4,128)}, u32[]{:S(2)}) copy-start(f32[3,4]{1,0:T(4,128)} %param.38) | copy-start | bytes 148
  197.9 1.5 copy-start.5
  197.9 1.5 copy-start.2
  197.9 1.5 copy-start.3
  198.0 1.5 copy-start.7
  198.0 17.5 %copy-start.11 = (f32[4,4]{1,0:T(4,128)S(1)}, f32[4,4]{1,0:T(4,128)}, u32[]{:S(2)}) copy-start(f32[4,4]{1,0:T(4,128)} %param.39) | copy-start | bytes 196
  199.5 15.8 %collective-permute-start = (f32[8,1,128]{2,1,0:T(1,128)S(1)}, f32[8,1,128]{2,1,0:T(1,128)S(1)}, u32[]{:S(2)}, u32[]{:S(2)}) collective-permute-start(f32[8,1,128]{2,1,0:T(1,128)S(1)} %get-tuple-element.20), channel_id=1, source_target_pairs={{0,1},{1,2},{2,3},{4,5},{5,6},{6,7},{8,9},{9,10},{10,11},{12,13},{... | collective-permute-start | bytes 12296 | tf_op jit(solution)/shard_map/ppermute | solution.py:447
  202.7 12.7 %collective-permute-start.1 = (f32[8,1,128]{2,1,0:T(1,128)S(1)}, f32[8,1,128]{2,1,0:T(1,128)S(1)}, u32[]{:S(2)}, u32[]{:S(2)}) collective-permute-start(f32[8,1,128]{2,1,0:T(1,128)S(1)} %get-tuple-element.21), channel_id=1, source_target_pairs={{1,0},{2,1},{3,2},{5,4},{6,5},{7,6},{9,8},{10,9},{11,10},{13,12},{... | collective-permute-start | bytes 12296 | tf_op jit(solution)/shard_map/ppermute | solution.py:448
  204.9 5.9 %collective-permute-start.2 = (f32[8,16,1]{2,1,0:T(8,128)S(1)}, f32[8,16,1]{2,1,0:T(8,128)S(1)}, u32[]{:S(2)}, u32[]{:S(2)}) collective-permute-start(f32[8,16,1]{2,1,0:T(8,128)S(1)} %get-tuple-element.22), channel_id=1, source_target_pairs={{0,4},{4,8},{8,12},{12,16},{16,20},{20,24},{24,28},{1,5},{5,9},{9,... | collective-permute-start | bytes 1544 | tf_op jit(solution)/shard_map/ppermute | solution.py:449
  208.9 6.5 %collective-permute-start.3 = (f32[8,16,1]{2,1,0:T(8,128)S(1)}, f32[8,16,1]{2,1,0:T(8,128)S(1)}, u32[]{:S(2)}, u32[]{:S(2)}) collective-permute-start(f32[8,16,1]{2,1,0:T(8,128)S(1)} %get-tuple-element.23), channel_id=1, source_target_pairs={{4,0},{8,4},{12,8},{16,12},{20,16},{24,20},{28,24},{5,1},{9,5},{13... | collective-permute-start | bytes 1544 | tf_op jit(solution)/shard_map/ppermute | solution.py:450
  215.5 0.7 copy-start
